TPU v7x, 512 devices: a whole 4x4x16 slice. The times are simulated.
512 devices in a mesh: blk: 32 (over z_lo, y), seq: 16 (over z_hi, x, core).
Axes of the slice: x: 4, y: 4, z: 16 (z_hi: 2, z_lo: 8; z = z_hi * 8 + z_lo), core: 2. Of those that a mesh axis runs over, the one named last changes fastest.
Arguments:
- tokens: bfloat16 [12288, 4096], P('seq', 'blk'), may hold values from -6 to 6
- grad_out: bfloat16 [12288, 4096], P('seq', 'blk'), may hold values from -0.0546875 to 0.0546875
- input_weight_blocks: bfloat16 [1024, 128, 128], P('blk'), may hold values from -0.25 to 0.25
- output_weight_blocks: bfloat16 [1024, 128, 128], P('blk'), may hold values from -0.25 to 0.25
- row_ids: int32 [1024], P('blk'), may hold values from 0 to 31, as said below
- lengths: int32 [16], P('seq'), may hold values from 1 to 768, 7680 in all
Outputs:
- grad_in: bfloat16 [1024, 128, 128], P('blk', 'seq')
- grad_w_out: bfloat16 [1024, 128, 128], P('blk', 'seq')
Inputs may be any that keep to these rules, and one draw needn't show every extreme that they name: `row_ids`: the 4 blocks of each hidden column block have distinct row blocks. `lengths`: some window is full.
All inputs are finite; a program needn't handle non-finite values. No bound on the sum of `lengths` on one device may be relied on, other than what follows from the above.
Results may differ from a plain program's by a relative error of at most 0.015.
Values may be sent and summed in bfloat16 or wider, within the bound.
No kernel may reach another device: no remote copies, remote signals or barrier semaphores. Data moves between devices by JAX's collectives and lax.ppermute only.
A program may use at most 64 MiB of HBM per device.

v0:
```python
import jax
import jax.numpy as jnp
from jax import lax
from jax.sharding import PartitionSpec as P

BLOCK_SIDE = 128
BLOCKS_PER_COLUMN = 4
gelu_scale = 0.7978845608


def gelu_pair(pre_act):
    tanh_val = jnp.tanh(gelu_scale * (pre_act + 0.044715 * pre_act * pre_act * pre_act))
    activation = 0.5 * pre_act * (1.0 + tanh_val)
    gelu_slope = 0.5 * (1.0 + tanh_val) + 0.5 * pre_act * (
        1.0 - tanh_val * tanh_val
    ) * gelu_scale * (1.0 + 0.134145 * pre_act * pre_act)
    return (activation, gelu_slope)


def shards(tokens, grad_out, input_weight_blocks, output_weight_blocks, row_ids, lengths):
    tok_rows = tokens.shape[0]
    groups = input_weight_blocks.shape[0] // BLOCKS_PER_COLUMN
    live_rows = lax.iota(jnp.int32, tok_rows)[:, None] < lengths[0]
    masked = jnp.where(live_rows, grad_out, jnp.zeros_like(grad_out))
    features = lax.all_gather(tokens, "blk", axis=1, tiled=True)
    x_slots = features.reshape(tok_rows, -1, BLOCK_SIDE)[:, row_ids, :]
    pre_slot = jnp.einsum(
        "tkc,kch->tkh", x_slots, input_weight_blocks, preferred_element_type=jnp.float32
    )
    pre_act = pre_slot.reshape(tok_rows, groups, BLOCKS_PER_COLUMN, BLOCK_SIDE).sum(2)
    activation, gelu_slope = gelu_pair(pre_act)
    activation = activation.astype(jnp.bfloat16)
    gradient = lax.all_gather(masked, "blk", axis=1, tiled=True)
    gradient_slots = gradient.reshape(tok_rows, -1, BLOCK_SIDE)[:, row_ids, :]
    g_four = gradient_slots.reshape(tok_rows, groups, BLOCKS_PER_COLUMN, BLOCK_SIDE)
    output_share = jnp.einsum(
        "tgh,tgrf->grhf", activation, g_four, preferred_element_type=jnp.float32
    )
    output_share = output_share.reshape(-1, BLOCK_SIDE, BLOCK_SIDE)
    slot_gradient = jnp.einsum(
        "xcn,cpn->xcp", gradient_slots, output_weight_blocks, preferred_element_type=jnp.float32
    )
    grad_act = slot_gradient.reshape(tok_rows, groups, BLOCKS_PER_COLUMN, BLOCK_SIDE).sum(2)
    grad_pre = (grad_act * gelu_slope).astype(jnp.bfloat16)
    x_four = x_slots.reshape(tok_rows, groups, BLOCKS_PER_COLUMN, BLOCK_SIDE)
    input_share = jnp.einsum("tgrc,tgh->grch", x_four, grad_pre, preferred_element_type=jnp.float32)
    input_share = input_share.reshape(-1, BLOCK_SIDE, BLOCK_SIDE)
    in_total, out_total = (
        lax.psum_scatter(
            input_share.astype(jnp.bfloat16), "seq", scatter_dimension=1, tiled=True
        ).astype(jnp.float32),
        lax.psum_scatter(
            output_share.astype(jnp.bfloat16), "seq", scatter_dimension=1, tiled=True
        ).astype(jnp.float32),
    )
    return (in_total.astype(jnp.bfloat16), out_total.astype(jnp.bfloat16))


def solution(mesh):
    return jax.shard_map(
        shards,
        mesh=mesh,
        in_specs=(
            P("seq", "blk"),
            P("seq", "blk"),
            P("blk", None, None),
            P("blk", None, None),
            P("blk"),
            P("seq"),
        ),
        out_specs=(P("blk", "seq", None), P("blk", "seq", None)),
        check_vma=False,
    )
```

profile of v0, /device:TPU:8, one launch (start us, length us, event | category | flops | bytes accessed | tf_op | source)
XLA Modules:
  0.0 731.5 jit_solution(1183288286320728725)
XLA Ops:
  7.2 1.8 copy.21
  9.8 1.1 copy.23
  10.9 0.7 broadcast_select_fusion
  11.6 0.7 compare_select_fusion
  12.3 235.6 %all-gather.3.cloned.1.call-done = bf16[768,4096]{0,1:T(8,128)(2,1)} async-done(((bf16[768,128]{0,1:T(8,128)(2,1)}), bf16[768,4096]{0,1:T(8,128)(2,1)}) %all-gather.3.cloned.1.call-update) | async-done | bytes 6291472 | tf_op jit(solution)/shard_map/all_gather | solution.py:25
  247.9 8.6 %copy.22 = bf16[768,32,128]{2,0,1:T(8,128)(2,1)} copy(bf16[768,32,128]{0,2,1:T(8,128)(2,1)} %bitcast.72) | data formatting | bytes 12582912 | tf_op jit(solution)/shard_map/reshape | solution.py:26
  256.5 225.1 %all-gather.5.cloned.1.call-done = bf16[768,4096]{0,1:T(8,128)(2,1)} async-done(((bf16[768,128]{0,1:T(8,128)(2,1)}), bf16[768,4096]{0,1:T(8,128)(2,1)}) %all-gather.5.cloned.1.call-update) | async-done | bytes 6291472 | tf_op jit(solution)/shard_map/all_gather | solution.py:33
  481.6 8.6 %copy.24 = bf16[768,32,128]{2,0,1:T(8,128)(2,1)} copy(bf16[768,32,128]{0,2,1:T(8,128)(2,1)} %bitcast.74) | data formatting | bytes 12582912 | tf_op jit(solution)/shard_map/reshape | solution.py:34
  490.2 6.8 gather_fusion
  496.9 6.8 gather_fusion.1
  503.7 4.9 bitcast_reduce_fusion
  508.7 2.9 fusion.30
  511.6 1.0 copy.34
  512.6 1.4 copy.45
  514.3 4.9 bitcast_reduce_fusion.1
  519.2 6.5 fusion.27
  525.7 0.7 copy.32
  526.4 1.4 copy.46
  527.8 92.1 %reduce-scatter.9.cloned.1.call-done = bf16[8,4096]{1,0:T(8,128)(2,1)} async-done(((bf16[128,4096]{1,0:T(8,128)(2,1)}), bf16[8,4096]{1,0:T(8,128)(2,1)}) %reduce-scatter.9.cloned.1.call-update) | async-done | bytes 65552
  619.9 0.8 copy.47
  620.7 0.7 copy.35
  621.4 102.0 %reduce-scatter.7.cloned.1.call-done = bf16[8,4096]{1,0:T(8,128)(2,1)} async-done(((bf16[128,4096]{1,0:T(8,128)(2,1)}), bf16[8,4096]{1,0:T(8,128)(2,1)}) %reduce-scatter.7.cloned.1.call-update) | async-done | bytes 65552
  723.4 0.8 copy.48
  724.3 0.7 copy.33
  (20 shorter events, 0.5 us)
Async XLA Ops:
  7.2 496.6 %copy-start = (bf16[32,128,128]{2,1,0:T(8,128)(2,1)S(1)}, bf16[32,128,128]{2,1,0:T(8,128)(2,1)}, u32[]{:S(2)}) copy-start(bf16[32,128,128]{2,1,0:T(8,128)(2,1)} %param.8) | copy-start | bytes 3145732
  7.2 240.7 %all-gather.3.cloned.1.call-start = ((), (), s32[]{:S(2)}) async-start(), calls=%async_computation.2 | async-start | bytes 6488064 | tf_op jit(solution)/shard_map/all_gather | solution.py:25
  9.1 472.5 %all-gather.5.cloned.1.call-start = ((), (), s32[]{:S(2)}) async-start(), calls=%async_computation.3 | async-start | bytes 6488064 | tf_op jit(solution)/shard_map/all_gather | solution.py:33
  11.6 608.3 %reduce-scatter.9.cloned.1.call-start = ((), (), s32[]{:S(2)}) async-start(), calls=%async_computation.5 | async-start | bytes 1114112
  503.7 4.9 copy-start.1
  508.7 2.9 copy-start.3
  512.5 1.7 copy-start.2
  514.0 209.4 %reduce-scatter.7.cloned.1.call-start = ((), (), s32[]{:S(2)}) async-start(), calls=%async_computation.4 | async-start | bytes 1114112
  514.2 5.0 copy-start.4
Sparse Core Ops, SparseCore 0:
  10.1 237.7 all-gather.2
  250.0 231.5 all-gather.4
  514.1 105.7 reduce-scatter.8
  625.1 98.2 reduce-scatter.6
where the time goes:
time: 732 us; the launch traced here: 731 us
  waiting for transfers between devices  655 us (89%)
  local copies, waits for them, and re-layouts  41.2 us (6%)
  matrix products  19.2 us (3%)
  between operations  14.5 us (2%)
    all_gather x1, waiting for transfers between devices, shards(): features = lax.all_gather(tokens, 'blk', axis=1, tiled=True)  236 us
    all_gather x1, waiting for transfers between devices, shards(): gradient = lax.all_gather(masked, 'blk', axis=1, tiled=True)  225 us
    unnamed x6, waiting for transfers between devices  194 us
  transfers between devices with their start and end apart: 4, of which 4 were waited for; matrix products, arithmetic and copies ran while one was open for 4% of the time, Pallas kernels for 0%

commit v1 on v0

--- a/solution.py
+++ b/solution.py
@@ -22,7 +22,9 @@
     groups = input_weight_blocks.shape[0] // BLOCKS_PER_COLUMN
     live_rows = lax.iota(jnp.int32, tok_rows)[:, None] < lengths[0]
     masked = jnp.where(live_rows, grad_out, jnp.zeros_like(grad_out))
-    features = lax.all_gather(tokens, "blk", axis=1, tiled=True)
+    features = jnp.concatenate(
+        lax.all_to_all(jnp.stack([tokens] * lax.axis_size("blk")), "blk", 0, 0), axis=1
+    )
     x_slots = features.reshape(tok_rows, -1, BLOCK_SIDE)[:, row_ids, :]
     pre_slot = jnp.einsum(
         "tkc,kch->tkh", x_slots, input_weight_blocks, preferred_element_type=jnp.float32

time: 732 us -> 638 us (0.87)
  waiting for transfers between devices: 655 us -> 548 us
  starting transfers between devices: 0.34 us -> 16.2 us
    all_gather x1 -> x0, waiting for transfers between devices: 236 us -> none  [shards(): features = lax.all_gather(tokens, 'blk', axis=1, tiled=True)]
    all_gather x1, waiting for transfers between devices: 225 us -> 316 us  [shards(): gradient = lax.all_gather(masked, 'blk', axis=1, tiled=True)]
    unnamed x6 -> x5, waiting for transfers between devices: 194 us -> 232 us
    all_to_all x0 -> x1, starting transfers between devices: none -> 15.9 us  [shards(): lax.all_to_all(jnp.stack([tokens] * lax.axis_size('blk')), 'blk', 0, 0)]
    reshape x1 -> x0, local copies, waits for them, and re-layouts: 8.62 us -> none  [shards(): x_slots = features.reshape(tok_rows, -1, BLOCK_SIDE)[:, row_ids, :]]
  transfers between devices with their start and end apart: 4 -> 4, of which waited for: 4 -> 3; matrix products, arithmetic and copies ran while one was open for 4% -> 5% of each run, Pallas kernels for 0% -> 0%
where the time goes in v1:
time: 638 us; the launch traced here: 637 us
  waiting for transfers between devices  548 us (86%)
  local copies, waits for them, and re-layouts  35.6 us (6%)
  matrix products  21.7 us (3%)
  starting transfers between devices  16.2 us (3%)
  between operations  14.5 us (2%)
    all_gather x1, waiting for transfers between devices, shards(): gradient = lax.all_gather(masked, 'blk', axis=1, tiled=True)  316 us
    unnamed x5, waiting for transfers between devices  232 us
    all_to_all x1, starting transfers between devices, shards(): lax.all_to_all(jnp.stack([tokens] * lax.axis_size('blk')), 'blk', 0, 0)  15.9 us
  transfers between devices with their start and end apart: 4, of which 3 were waited for; matrix products, arithmetic and copies ran while one was open for 5% of the time, Pallas kernels for 0%

profile of v1, /device:TPU:8, one launch (start us, length us, event | category | flops | bytes accessed | tf_op | source)
XLA Modules:
  0.0 637.2 jit_solution(9291599465245371389)
XLA Ops:
  7.2 5.0 stack.2
  12.2 15.9 %all-to-all-start = ((bf16[32,768,128]{2,1,0:T(8,128)(2,1)}), bf16[32,768,128]{2,1,0:T(8,128)(2,1)}, u32[]{:S(2)}, u32[]{:S(2)}) async-start(bf16[32,768,128]{2,1,0:T(8,128)(2,1)} %stack.2), calls=%async_computation | async-start | bytes 12582912 | tf_op jit(solution)/shard_map/all_to_all | solution.py:26
  28.2 0.1 copy.20
  29.0 0.7 broadcast_select_fusion
  29.8 316.5 %all-gather.2.cloned.1.call-done = bf16[768,4096]{0,1:T(8,128)(2,1)} async-done(((bf16[768,128]{0,1:T(8,128)(2,1)}), bf16[768,4096]{0,1:T(8,128)(2,1)}) %all-gather.2.cloned.1.call-update) | async-done | bytes 6291472 | tf_op jit(solution)/shard_map/all_gather | solution.py:35
  346.3 8.7 %copy.21 = bf16[768,32,128]{2,0,1:T(8,128)(2,1)} copy(bf16[768,32,128]{0,2,1:T(8,128)(2,1)} %bitcast.74) | data formatting | bytes 12582912 | tf_op jit(solution)/shard_map/reshape | solution.py:36
  355.0 6.8 %gather_fusion.1 = bf16[32,768,128]{2,1,0:T(8,128)(2,1)} fusion(bf16[768,32,128]{2,0,1:T(8,128)(2,1)} %copy.21, s32[1024]{0:T(1024)S(1)} %pad_clamp_fusion), kind=kCustom, calls=%fused_computation.1 | custom fusion | bytes 12583040 | tf_op jit(solution)/shard_map/gather | solution.py:36
  361.8 6.4 %bitcast_reduce_fusion.1 = f32[768,8,128]{2,0,1:T(8,128)} fusion(bf16[32,128,128]{2,1,0:T(8,128)(2,1)S(1)} %copy-done, bf16[32,768,128]{2,1,0:T(8,128)(2,1)} %gather_fusion.1), kind=kOutput, calls=%fused_computation.3 | convolution fusion | flops 807665664 | bytes 10485760 | tf_op jit(solution)/shard_map/xcn,cpn->xcp/dot_general | solution.py:42
  368.2 6.8 %gather_fusion = bf16[32,768,128]{2,1,0:T(8,128)(2,1)} fusion(bf16[768,32,128]{2,0,1:T(8,128)(2,1)} %bitcast, s32[1024]{0:T(1024)S(1)} %pad_clamp_fusion), kind=kCustom, calls=%fused_computation | custom fusion | bytes 12583040 | tf_op jit(solution)/shard_map/gather | solution.py:28
  375.1 4.9 bitcast_reduce_fusion
  380.0 0.5 copy-done.6
  380.6 3.9 fusion.27
  384.5 0.7 copy.27
  385.2 1.4 copy.41
  386.7 0.2 reduce-scatter.9.cloned.1.call-start
  386.9 6.5 %fusion.30 = bf16[8,4,128,128]{3,2,1,0:T(8,128)(2,1)S(1)} fusion(bf16[768,8,4,128]{3,0,2,1:T(8,128)(2,1)} %bitcast.73, f32[768,8,128]{2,0,1:T(8,128)} %copy-done.5), kind=kOutput, calls=%fused_computation.30 | convolution fusion | flops 812908544 | bytes 10485760 | tf_op jit(solution)/shard_map/tgh,tgrf->grhf/dot_general | solution.py:38
  393.3 1.0 copy.29
  394.3 1.4 copy.40
  395.8 129.7 %reduce-scatter.7.cloned.1.call-done = bf16[8,4096]{1,0:T(8,128)(2,1)} async-done(((bf16[128,4096]{1,0:T(8,128)(2,1)}), bf16[8,4096]{1,0:T(8,128)(2,1)}) %reduce-scatter.7.cloned.1.call-update) | async-done | bytes 65552
  525.5 0.8 copy.43
  526.3 0.7 copy.28
  527.0 102.2 %reduce-scatter.9.cloned.1.call-done = bf16[8,4096]{1,0:T(8,128)(2,1)} async-done(((bf16[128,4096]{1,0:T(8,128)(2,1)}), bf16[8,4096]{1,0:T(8,128)(2,1)}) %reduce-scatter.9.cloned.1.call-update) | async-done | bytes 65552
  629.2 0.8 copy.42
  630.1 0.7 copy.30
  (22 shorter events, 0.2 us)
Async XLA Ops:
  7.2 354.6 %copy-start = (bf16[32,128,128]{2,1,0:T(8,128)(2,1)S(1)}, bf16[32,128,128]{2,1,0:T(8,128)(2,1)}, u32[]{:S(2)}) copy-start(bf16[32,128,128]{2,1,0:T(8,128)(2,1)} %param.9) | copy-start | bytes 3145732
  12.2 16.0 %copy-start.2 = (bf16[768,128]{1,0:T(8,128)(2,1)S(1)}, bf16[768,128]{1,0:T(8,128)(2,1)}, u32[]{:S(2)}) copy-start(bf16[768,128]{1,0:T(8,128)(2,1)} %param.7) | copy-start | bytes 589828
  12.2 17.6 %copy-start.4 = (s32[32]{0:T(128)S(1)}, s32[32]{0:T(128)}, u32[]{:S(2)}) copy-start(s32[32]{0:T(128)} %param.10) | copy-start | bytes 388
  12.2 356.0 %all-to-all-start = ((bf16[32,768,128]{2,1,0:T(8,128)(2,1)}), bf16[32,768,128]{2,1,0:T(8,128)(2,1)}, u32[]{:S(2)}, u32[]{:S(2)}) async-start(bf16[32,768,128]{2,1,0:T(8,128)(2,1)} %stack.2), calls=%async_computation | async-start | bytes 12582912 | tf_op jit(solution)/shard_map/all_to_all | solution.py:26
  28.2 318.2 %all-gather.2.cloned.1.call-start = ((), (), s32[]{:S(2)}) async-start(), calls=%async_computation.3 | async-start | bytes 6488064 | tf_op jit(solution)/shard_map/all_gather | solution.py:35
  29.8 495.7 %reduce-scatter.7.cloned.1.call-start = ((), (), s32[]{:S(2)}) async-start(), calls=%async_computation.4 | async-start | bytes 1114112
  368.2 6.8 %copy-start.3 = (bf16[32,128,128]{2,1,0:T(8,128)(2,1)S(1)}, bf16[32,128,128]{2,1,0:T(8,128)(2,1)}, u32[]{:S(2)}) copy-start(bf16[32,128,128]{2,1,0:T(8,128)(2,1)} %param.8) | copy-start | bytes 3145732
  375.1 5.0 copy-start.1
  375.1 5.5 copy-start.6
  380.0 4.5 copy-start.5
  386.7 242.5 %reduce-scatter.9.cloned.1.call-start = ((), (), s32[]{:S(2)}) async-start(), calls=%async_computation.5 | async-start | bytes 1114112
Sparse Core Ops, SparseCore 0:
  31.1 315.1 all-gather.1
  386.8 138.6 reduce-scatter.6
  530.9 98.2 reduce-scatter.8
